TPU v7x, 256 devices: a whole 4x4x8 slice. The times are simulated.
256 devices in a mesh: gz: 16 (over y, x), dom: 16 (over z, core).
Axes of the slice: x: 4, y: 4, z: 8, core: 2. Of those that a mesh axis runs over, the one named last changes fastest.
Arguments:
- volume: float32 [768, 4, 384], P('gz'), may hold values from -6 to 6
- observed: bfloat16 [4096, 4, 384], P(('gz', 'dom')), may hold values from -6 to 6
- ctf_table: float32 [32, 2, 384], replicated, may hold values from -1 to 1
- ctf_class: int32 [4096], P(('gz', 'dom')), may hold values from 0 to 31
- bin_ids: int32 [4096], P(('gz', 'dom')), may hold values from 0 to 127
Outputs:
- pose_score: float32 [4096], P(('gz', 'dom'))
- backprojection: float32 [768, 4, 384], P(('gz', 'dom'))
All inputs are finite; a program needn't handle non-finite values.
Results may differ from a plain program's by a relative error of at most 0.0034.
Values may be sent and summed in bfloat16 or wider, within the bound.
A program may use at most 64 MiB of HBM per device.

v0:
```python
import math
import jax
import jax.numpy as jnp
from jax import lax
from jax.sharding import PartitionSpec as P

NZ = 768
NB_DEV = 8
NCTF = 32
ITERS = 3
epsilon = 1e-05


def kernel(offset):
    inside = jnp.abs(offset) < 1.0
    falloff = 1.0 - offset * offset
    return (
        jnp.where(inside, falloff * falloff, 0.0),
        jnp.where(inside, -4.0 * offset * falloff, 0.0),
    )


def geometry(bin_index, planes, total_bins, samples, columns):
    tilt_angle = -0.5 * math.pi + math.pi * (bin_index.astype(jnp.float32) + 0.5) / total_bins
    sine_value = jnp.sin(tilt_angle)
    cosine = jnp.cos(tilt_angle)
    radius = jnp.arange(samples).astype(jnp.float32)
    centre = 0.5 * NZ + radius * sine_value
    z_value, z_slope = kernel(planes[None, :] - centre[:, None])
    z_slope = z_slope * (-radius * cosine / samples)[:, None]
    x_value, x_slope = kernel(
        jnp.arange(columns).astype(jnp.float32)[None, :] - (radius * cosine)[:, None]
    )
    x_slope = x_slope * (radius * sine_value / samples)[:, None]
    return (z_value, z_slope, jnp.concatenate([x_value, x_slope], 0))


def contrast_of(classes, ctf_table, count, stacked_rows, samples):
    class_onehot = (classes[:, None] == jnp.arange(NCTF, dtype=jnp.int32)[None, :]).astype(
        jnp.float32
    )
    contrast = jnp.dot(
        class_onehot,
        ctf_table.reshape(NCTF, -1),
        precision=lax.Precision.HIGHEST,
        preferred_element_type=jnp.float32,
    )
    contrast = contrast.reshape(count, stacked_rows // 2, samples)
    return jnp.concatenate([contrast, contrast], 1)


def local(volume, observed, ctf_table, ctf_class, bin_ids):
    depth_local = volume.shape[0]
    stacked_rows = volume.shape[1]
    columns = volume.shape[2]
    samples = observed.shape[2]
    particles = observed.shape[0]
    total_bins = NB_DEV * lax.axis_size("dom")
    first_bin = lax.axis_index("dom") * NB_DEV
    planes = (lax.axis_index("gz") * depth_local + jnp.arange(depth_local, dtype=jnp.int32)).astype(
        jnp.float32
    )
    flat_volume = volume.reshape(depth_local * stacked_rows, columns)

    def extract(offset):
        z_value, z_slope, x_weights = geometry(
            first_bin + offset, planes, total_bins, samples, columns
        )
        resampled = jnp.dot(
            flat_volume,
            x_weights.T,
            precision=lax.Precision.HIGHEST,
            preferred_element_type=jnp.float32,
        )
        resampled = resampled.reshape(depth_local, stacked_rows, 2 * samples)
        direct = resampled[:, :, :samples]
        tilted = resampled[:, :, samples:]
        leading = jnp.sum(direct * z_value.T[:, None, :], axis=0)
        second = jnp.sum(direct * z_slope.T[:, None, :] + tilted * z_value.T[:, None, :], axis=0)
        return jnp.concatenate([leading, second], 0)

    partial_slices = lax.map(extract, jnp.arange(NB_DEV, dtype=jnp.int32))
    reduced = lax.psum(partial_slices, "gz")
    gathered = lax.all_gather(reduced.astype(jnp.bfloat16), "dom", axis=0, tiled=True)
    bin_onehot = bin_ids[:, None] == jnp.arange(total_bins, dtype=jnp.int32)[None, :]
    picked = jnp.dot(
        bin_onehot.astype(jnp.bfloat16),
        gathered.reshape(total_bins, -1),
        preferred_element_type=jnp.float32,
    )
    picked = picked.reshape(particles, 2 * stacked_rows, samples)
    contrast = contrast_of(ctf_class, ctf_table, particles, stacked_rows, samples)
    measured = observed.astype(jnp.float32)
    predicted = contrast * picked[:, :stacked_rows]
    tangent = contrast * picked[:, stacked_rows:]
    curvature = jnp.sum(tangent * tangent, axis=(1, 2)) + epsilon
    shift = jnp.zeros((particles,), jnp.float32)
    for iteration in range(ITERS):
        residual_map = measured - predicted - shift[:, None, None] * tangent
        shift = shift + 0.5 * jnp.sum(residual_map * tangent, axis=(1, 2)) / curvature
    pose_score = shift * jnp.sqrt(curvature)
    onehot_float = bin_onehot.astype(jnp.float32)
    weighted = contrast * measured
    contributions = jnp.concatenate([weighted, shift[:, None, None] * weighted], 1).reshape(
        particles, -1
    )
    totals = jnp.dot(
        onehot_float.T,
        contributions,
        precision=lax.Precision.HIGHEST,
        preferred_element_type=jnp.float32,
    )
    totals = lax.psum(totals, ("gz", "dom"))
    owned = lax.dynamic_slice_in_dim(totals, first_bin, NB_DEV, 0)
    owned = owned.reshape(NB_DEV, 2 * stacked_rows, samples)

    def spread_back(offset, accumulated):
        z_value, z_slope, x_weights = geometry(
            first_bin + offset, planes, total_bins, samples, columns
        )
        summed = lax.dynamic_index_in_dim(owned, offset, 0, keepdims=False)
        direct = summed[:stacked_rows]
        tilted = summed[stacked_rows:]
        z_plain = z_value.T[:, None, :]
        z_tilted = z_slope.T[:, None, :]
        leading = z_plain * direct[None] + z_tilted * tilted[None]
        second = z_plain * tilted[None]
        stacked = jnp.concatenate([leading, second], 2).reshape(
            depth_local * stacked_rows, 2 * samples
        )
        return accumulated + jnp.dot(
            stacked, x_weights, precision=lax.Precision.HIGHEST, preferred_element_type=jnp.float32
        )

    backprojected = lax.fori_loop(
        0, NB_DEV, spread_back, jnp.zeros((depth_local * stacked_rows, columns), jnp.float32)
    )
    backprojected = backprojected.reshape(depth_local, stacked_rows, columns)
    plane_share = lax.psum_scatter(backprojected, "dom", scatter_dimension=0, tiled=True)
    return (pose_score, plane_share)


def solution(mesh):
    return jax.shard_map(
        local,
        mesh=mesh,
        in_specs=(
            P("gz", None, None),
            P(("gz", "dom"), None, None),
            P(),
            P(("gz", "dom")),
            P(("gz", "dom")),
        ),
        out_specs=(P(("gz", "dom")), P(("gz", "dom"), None, None)),
        check_vma=False,
    )
```

profile of v0, /device:TPU:1, one launch (start us, length us, event | category | flops | bytes accessed | tf_op | source)
XLA Modules:
  0.0 525.4 jit_solution(10506065352268123500)
XLA Ops:
  7.2 1.1 reshape.295
  8.3 28.8 %while.29 = (s32[]{:T(128)}, f32[8,8,384]{2,1,0:T(8,128)S(1)}, s32[8]{0:T(128)S(1)}, s32[]{:T(128)}, f32[192,384]{1,0:T(8,128)S(1)}, /*index=5*/s32[]{:T(128)}, s32[]{:T(128)}, f32[]{:T(128)}, f32[]{:T(128)}, f32[]{:T(128)}) while((s32[]{:T(128)}, f32[8,8,384]{2,1,0:T(8,128)S(1)}, s32[8]{0:T(128)S(1)}, s32[]{:T(128)}, ...), condition=%wide.region_3.4_spmd.clone, body=%wide.region_0.3_spmd.clone.sunk | while | flops 682043264 | bytes 5361225 | solution.py:82
  8.3 0.6 dynamic_slice.26
  9.7 0.3 fusion.88
  10.0 1.4 convolution_bitcast_fusion.2
  11.9 0.6 dynamic_slice.26
  13.2 0.3 fusion.88
  13.5 1.5 convolution_bitcast_fusion.2
  15.5 0.6 dynamic_slice.26
  16.9 0.3 fusion.88
  17.2 1.4 convolution_bitcast_fusion.2
  19.1 0.6 dynamic_slice.26
  20.5 0.3 fusion.88
  20.7 1.5 convolution_bitcast_fusion.2
  22.7 0.6 dynamic_slice.26
  24.1 0.3 fusion.88
  24.4 1.4 convolution_bitcast_fusion.2
  26.3 0.6 dynamic_slice.26
  27.7 0.3 fusion.88
  28.0 1.5 convolution_bitcast_fusion.2
  29.9 0.6 dynamic_slice.26
  31.3 0.3 fusion.88
  31.6 1.4 convolution_bitcast_fusion.2
  33.5 0.6 dynamic_slice.26
  34.9 0.3 fusion.88
  35.2 1.5 convolution_bitcast_fusion.2
  37.2 62.0 %psum.14 = bf16[8,8,384]{2,1,0:T(8,128)(2,1)S(1)} all-reduce(f32[8,8,384]{2,1,0:T(8,128)S(1)} %get-tuple-element.211), channel_id=1, replica_groups=mesh['gz'=16,'dom'=16] {'gz'}, use_global_device_ids=true, to_apply=%region_4.5 | all-reduce | flops 24576 | bytes 147456 | tf_op jit(solution)/shard_map/psum | solution.py:83
  99.1 36.8 %all_gather.3 = bf16[128,8,384]{2,1,0:T(8,128)(2,1)S(1)} all-gather(bf16[8,8,384]{2,1,0:T(8,128)(2,1)S(1)} %psum.14), channel_id=1, replica_groups=mesh['gz'=16,'dom'=16] {'dom'}, dimensions={0}, use_global_device_ids=true | all-gather | bytes 835584 | tf_op jit(solution)/shard_map/all_gather | solution.py:84
  136.0 0.6 copy.17
  136.6 0.3 fusion.58
  137.7 0.5 sqrt_multiply_fusion
  138.4 2.0 fusion.63
  140.5 251.3 %all-reduce.4.cloned.1.call-done = f32[128,3072]{1,0:T(8,128)} async-done(((f32[128,3072]{1,0:T(8,128)}), f32[128,3072]{1,0:T(8,128)}) %all-reduce.4.cloned.1.call-update) | async-done | bytes 1572880 | tf_op jit(solution)/shard_map/psum | solution.py:113
  391.8 0.9 constant_dynamic-slice_fusion.1
  392.7 17.9 %while.30 = (s32[]{:T(128)}, f32[192,384]{1,0:T(8,128)S(1)}, s32[]{:T(128)}, f32[8,8,384]{2,1,0:T(8,128)S(1)}, s32[]{:T(128)}, /*index=5*/s32[]{:T(128)}, f32[]{...) while((s32[]{:T(128)}, f32[192,384]{1,0:T(8,128)S(1)}, s32[]{:T(128)}, ...), condition=%wide.region_11.12_spmd.clone, body=%wide.region_10.11_spmd.clone.sunk | while | flops 682190720 | bytes 5656159 | solution.py:135
  393.7 1.2 fusion.96
  395.9 1.2 fusion.96
  398.2 1.2 fusion.96
  400.4 1.2 fusion.96
  402.3 0.3 fusion.94
  402.6 1.2 fusion.96
  404.9 1.2 fusion.96
  407.1 1.2 fusion.96
  409.4 1.2 fusion.96
  410.6 0.8 reshape.299
  411.4 0.6 dynamic-slice
  412.7 104.5 %all-reduce.6.cloned.1.call-done = f32[48,4,384]{2,1,0:T(4,128)} async-done(((f32[48,4,384]{2,1,0:T(4,128)}), f32[48,4,384]{2,1,0:T(4,128)}) %all-reduce.6.cloned.1.call-update) | async-done | bytes 294928
  517.2 1.3 constant_dynamic-slice_fusion
  (170 shorter events, 10.4 us)
Async XLA Ops:
  7.2 384.6 %all-reduce.4.cloned.1.call-start = ((), (), s32[]{:S(2)}) async-start(), calls=%async_computation | async-start | bytes 3145728 | tf_op jit(solution)/shard_map/psum | solution.py:113
  99.1 37.5 %copy-start.2 = (s32[16]{0:T(128)S(1)}, s32[16]{0:T(128)}, u32[]{:S(2)}) copy-start(s32[16]{0:T(128)} %param.13) | copy-start | bytes 196
  136.0 0.9 copy-start.1
  136.0 1.0 copy-start.3
  136.0 1.2 copy-start
  140.4 376.8 %all-reduce.6.cloned.1.call-start = ((), (), s32[]{:S(2)}) async-start(), calls=%async_computation.1 | async-start | bytes 589824
  392.7 18.7 %copy-start.4 = (u32[256]{0:T(256)S(1)}, u32[256]{0:T(256)}, u32[]{:S(2)}) copy-start(u32[256]{0:T(256)} %constant.211) | copy-start | bytes 3076
Sparse Core Ops, SparseCore 0:
  140.6 251.1 all-reduce.3
  411.6 105.6 all-reduce.5
where the time goes:
time: 526 us; the launch traced here: 525 us
  waiting for transfers between devices  356 us (68%)
  blocking collectives  98.8 us (19%)
  matrix products  24.2 us (5%)
  between operations  14.8 us (3%)
  local copies, waits for them, and re-layouts  13.1 us (2%)
  other arithmetic  10.1 us (2%)
  loops' own time  8.51 us (2%)
    psum x1, waiting for transfers between devices, local(): totals = lax.psum(totals, ('gz', 'dom'))  251 us
    unnamed x3, waiting for transfers between devices  105 us
    psum x1, blocking collectives, local(): reduced = lax.psum(partial_slices, 'gz')  62 us
    all_gather x1, blocking collectives, local(): lax.all_gather(reduced.astype(jnp.bfloat16), 'dom', axis=0, tiled=True)  36.8 us
    dot_general x8, matrix products, extract(): jnp.dot(flat_volume, x_weights.T, precision=lax.Precision.HIGHEST, prefer...  11.7 us
  transfers between devices with their start and end apart: 2, of which 2 were waited for; matrix products, arithmetic and copies ran while one was open for 0% of the time, Pallas kernels for 0%

commit v1 on v0

--- a/solution.py
+++ b/solution.py
@@ -81,7 +81,9 @@
 
     partial_slices = lax.map(extract, jnp.arange(NB_DEV, dtype=jnp.int32))
     reduced = lax.psum(partial_slices, "gz")
-    gathered = lax.all_gather(reduced.astype(jnp.bfloat16), "dom", axis=0, tiled=True)
+    shard = reduced.astype(jnp.bfloat16)
+    copies = jnp.concatenate([shard] * lax.axis_size("dom"), axis=0)
+    gathered = lax.all_to_all(copies, "dom", 0, 0, tiled=True)
     bin_onehot = bin_ids[:, None] == jnp.arange(total_bins, dtype=jnp.int32)[None, :]
     picked = jnp.dot(
         bin_onehot.astype(jnp.bfloat16),

time: 526 us -> 545 us (1.036)
  blocking collectives: 98.8 us -> 62.1 us
  starting transfers between devices: 0.08 us -> 23.4 us
  waiting for transfers between devices: 356 us -> 378 us
  local copies, waits for them, and re-layouts: 13.1 us -> 23.5 us
    all_gather x1 -> x0, blocking collectives: 36.8 us -> none  [local(): lax.all_gather(reduced.astype(jnp.bfloat16), 'dom', axis=0, tiled=True)]
    all_to_all x0 -> x1, starting transfers between devices: none -> 23.4 us  [local(): gathered = lax.all_to_all(copies, 'dom', 0, 0, tiled=True)]
    all_to_all x0 -> x1, waiting for transfers between devices: none -> 22.4 us  [local(): gathered = lax.all_to_all(copies, 'dom', 0, 0, tiled=True)]
    unnamed x13 -> x28, local copies, waits for them, and re-layouts: 1.96 us -> 11.2 us
  transfers between devices with their start and end apart: 2 -> 3, of which waited for: 2 -> 3; matrix products, arithmetic and copies ran while one was open for 0% -> 0% of each run, Pallas kernels for 0% -> 0%
where the time goes in v1:
time: 545 us
  waiting for transfers between devices  378 us (69%)
  blocking collectives  62.1 us (11%)
  matrix products  24 us (4%)
  local copies, waits for them, and re-layouts  23.5 us (4%)
  starting transfers between devices  23.4 us (4%)
  between operations  14.8 us (3%)
  other arithmetic  10.1 us (2%)
  loops' own time  9.1 us (2%)
    psum x1, waiting for transfers between devices, local(): totals = lax.psum(totals, ('gz', 'dom'))  251 us
    unnamed x3, waiting for transfers between devices  105 us
    psum x1, blocking collectives, local(): reduced = lax.psum(partial_slices, 'gz')  62.1 us
    all_to_all x1, starting transfers between devices, local(): gathered = lax.all_to_all(copies, 'dom', 0, 0, tiled=True)  23.4 us
    all_to_all x1, waiting for transfers between devices, local(): gathered = lax.all_to_all(copies, 'dom', 0, 0, tiled=True)  22.4 us
    dot_general x8, matrix products, extract(): jnp.dot(flat_volume, x_weights.T, precision=lax.Precision.HIGHEST, prefer...  11.5 us
    unnamed x28, local copies, waits for them, and re-layouts  11.2 us
  transfers between devices with their start and end apart: 3, of which 3 were waited for; matrix products, arithmetic and copies ran while one was open for 0% of the time, Pallas kernels for 0%

profile of v1, /device:TPU:1, one launch (start us, length us, event | category | flops | bytes accessed | tf_op | source)
XLA Modules:
  0.0 544.7 jit_solution(13719288564388880567)
XLA Ops:
  7.2 1.1 reshape.295
  8.3 29.8 %while.29 = (s32[]{:T(128)}, f32[8,8,384]{2,1,0:T(8,128)S(1)}, s32[8]{0:T(128)S(1)}, s32[]{:T(128)}, f32[192,384]{1,0:T(8,128)S(1)}, /*index=5*/s32[]{:T(128)}, s32[]{:T(128)}, f32[]{:T(128)}, f32[]{:T(128)}, f32[]{:T(128)}) while((s32[]{:T(128)}, f32[8,8,384]{2,1,0:T(8,128)S(1)}, s32[8]{0:T(128)S(1)}, s32[]{:T(128)}, ...), condition=%wide.region_3.4_spmd.clone, body=%wide.region_0.3_spmd.clone.sunk | while | flops 682043264 | bytes 5361225 | solution.py:82
  8.3 0.7 dynamic_slice.26
  10.1 1.4 convolution_bitcast_fusion.2
  12.0 0.7 dynamic_slice.26
  13.8 1.4 convolution_bitcast_fusion.2
  15.7 0.7 dynamic_slice.26
  17.5 1.4 convolution_bitcast_fusion.2
  19.4 0.7 dynamic_slice.26
  21.2 1.4 convolution_bitcast_fusion.2
  23.2 0.7 dynamic_slice.26
  25.0 1.4 convolution_bitcast_fusion.2
  26.9 0.7 dynamic_slice.26
  28.7 1.4 convolution_bitcast_fusion.2
  30.6 0.7 dynamic_slice.26
  32.4 1.4 convolution_bitcast_fusion.2
  34.3 0.7 dynamic_slice.26
  36.1 1.4 convolution_bitcast_fusion.2
  38.1 62.1 %psum.14 = bf16[8,8,384]{2,1,0:T(8,128)(2,1)S(1)} all-reduce(f32[8,8,384]{2,1,0:T(8,128)S(1)} %get-tuple-element.211), channel_id=1, replica_groups=mesh['gz'=16,'dom'=16] {'gz'}, use_global_device_ids=true, to_apply=%region_4.5 | all-reduce | flops 24576 | bytes 147456 | tf_op jit(solution)/shard_map/psum | solution.py:83
  100.2 0.6 constant_dynamic-update-slice_fusion.15
  100.8 0.6 constant_dynamic-update-slice_fusion.14
  101.4 0.6 constant_dynamic-update-slice_fusion.13
  102.0 0.6 constant_dynamic-update-slice_fusion.12
  103.3 0.6 constant_dynamic-update-slice_fusion.10
  104.5 0.6 constant_dynamic-update-slice_fusion.8
  106.4 0.6 constant_dynamic-update-slice_fusion.5
  107.0 0.6 constant_dynamic-update-slice_fusion.4
  107.6 0.6 constant_dynamic-update-slice_fusion.3
  108.2 0.6 constant_dynamic-update-slice_fusion.2
  108.9 0.6 constant_dynamic-update-slice_fusion.1
  109.5 0.6 constant_dynamic-update-slice_fusion
  110.1 23.4 %all-to-all-start = ((bf16[128,8,384]{2,1,0:T(8,128)(2,1)}), bf16[128,8,384]{2,1,0:T(8,128)(2,1)S(1)}, u32[]{:S(2)}, u32[]{:S(2)}) async-start(bf16[128,8,384]{2,1,0:T(8,128)(2,1)} %constant_dynamic-update-slice_fusion), calls=%async_computation | async-start | bytes 1572864 | tf_op jit(solution)/shard_map/all_to_all | solution.py:86
  133.8 22.4 %all-to-all-done = bf16[128,8,384]{2,1,0:T(8,128)(2,1)S(1)} async-done(((bf16[128,8,384]{2,1,0:T(8,128)(2,1)}), bf16[128,8,384]{2,1,0:T(8,128)(2,1)S(1)}, u32[]{:S(2)}, u32[]{:S(2)}) %all-to-all-start) | async-done | bytes 786464 | tf_op jit(solution)/shard_map/all_to_all | solution.py:86
  158.3 2.1 fusion.63
  160.4 250.7 %all-reduce.4.cloned.1.call-done = f32[128,3072]{1,0:T(8,128)} async-done(((f32[128,3072]{1,0:T(8,128)}), f32[128,3072]{1,0:T(8,128)}) %all-reduce.4.cloned.1.call-update) | async-done | bytes 1572880 | tf_op jit(solution)/shard_map/psum | solution.py:115
  411.1 0.9 constant_dynamic-slice_fusion.1
  412.0 17.9 %while.30 = (s32[]{:T(128)}, f32[192,384]{1,0:T(8,128)S(1)}, s32[]{:T(128)}, f32[8,8,384]{2,1,0:T(8,128)S(1)}, s32[]{:T(128)}, /*index=5*/s32[]{:T(128)}, f32[]{...) while((s32[]{:T(128)}, f32[192,384]{1,0:T(8,128)S(1)}, s32[]{:T(128)}, ...), condition=%wide.region_11.12_spmd.clone, body=%wide.region_10.11_spmd.clone.sunk | while | flops 682190720 | bytes 5656159 | solution.py:137
  413.0 1.2 fusion.96
  415.2 1.2 fusion.96
  417.5 1.2 fusion.96
  419.7 1.2 fusion.96
  422.0 1.2 fusion.96
  424.2 1.2 fusion.96
  426.4 1.2 fusion.96
  428.7 1.2 fusion.96
  429.9 0.8 reshape.299
  432.0 104.5 %all-reduce.6.cloned.1.call-done = f32[48,4,384]{2,1,0:T(4,128)} async-done(((f32[48,4,384]{2,1,0:T(4,128)}), f32[48,4,384]{2,1,0:T(4,128)}) %all-reduce.6.cloned.1.call-update) | async-done | bytes 294928
  536.5 1.3 constant_dynamic-slice_fusion
  (187 shorter events, 17.5 us)
Async XLA Ops:
  105.1 28.4 %copy-start.1 = (f32[32,2,384]{2,1,0:T(2,128)S(1)}, f32[32,2,384]{2,1,0:T(2,128)}, u32[]{:S(2)}) copy-start(f32[32,2,384]{2,1,0:T(2,128)} %param.11) | copy-start | bytes 294916
  105.1 28.4 %copy-start.3 = (s32[16]{0:T(128)S(1)}, s32[16]{0:T(128)}, u32[]{:S(2)}) copy-start(s32[16]{0:T(128)} %param.12) | copy-start | bytes 196
  110.1 46.0 %all-to-all-start = ((bf16[128,8,384]{2,1,0:T(8,128)(2,1)}), bf16[128,8,384]{2,1,0:T(8,128)(2,1)S(1)}, u32[]{:S(2)}, u32[]{:S(2)}) async-start(bf16[128,8,384]{2,1,0:T(8,128)(2,1)} %constant_dynamic-update-slice_fusion), calls=%async_computation | async-start | bytes 1572864 | tf_op jit(solution)/shard_map/all_to_all | solution.py:86
  133.5 23.2 %copy-start.2 = (s32[16]{0:T(128)S(1)}, s32[16]{0:T(128)}, u32[]{:S(2)}) copy-start(s32[16]{0:T(128)} %param.13) | copy-start | bytes 196
  133.5 277.6 %all-reduce.4.cloned.1.call-start = ((), (), s32[]{:S(2)}) async-start(), calls=%async_computation.1 | async-start | bytes 3145728 | tf_op jit(solution)/shard_map/psum | solution.py:115
  133.8 23.3 %copy-start = (bf16[16,4,384]{2,1,0:T(4,128)(2,1)S(1)}, bf16[16,4,384]{2,1,0:T(4,128)(2,1)}, u32[]{:S(2)}) copy-start(bf16[16,4,384]{2,1,0:T(4,128)(2,1)} %param.10) | copy-start | bytes 147460
  160.4 376.2 %all-reduce.6.cloned.1.call-start = ((), (), s32[]{:S(2)}) async-start(), calls=%async_computation.2 | async-start | bytes 589824
  412.0 18.8 %copy-start.4 = (u32[256]{0:T(256)S(1)}, u32[256]{0:T(256)}, u32[]{:S(2)}) copy-start(u32[256]{0:T(256)} %constant.211) | copy-start | bytes 3076
Sparse Core Ops, SparseCore 0:
  160.5 250.5 all-reduce.3
  430.9 105.6 all-reduce.5

commit v2 on v0

--- a/solution.py
+++ b/solution.py
@@ -80,7 +80,7 @@
         return jnp.concatenate([leading, second], 0)
 
     partial_slices = lax.map(extract, jnp.arange(NB_DEV, dtype=jnp.int32))
-    reduced = lax.psum(partial_slices, "gz")
+    reduced = jnp.sum(lax.all_gather(partial_slices, "gz"), axis=0)
     gathered = lax.all_gather(reduced.astype(jnp.bfloat16), "dom", axis=0, tiled=True)
     bin_onehot = bin_ids[:, None] == jnp.arange(total_bins, dtype=jnp.int32)[None, :]
     picked = jnp.dot(

time: 526 us -> 505 us (0.960)
  blocking collectives: 98.8 us -> 21 us
  waiting for transfers between devices: 356 us -> 410 us
    psum x1 -> x0, blocking collectives: 62 us -> none  [local(): reduced = lax.psum(partial_slices, 'gz')]
    all_gather x0 -> x1, waiting for transfers between devices: none -> 51.7 us  [local(): reduced = jnp.sum(lax.all_gather(partial_slices, 'gz'), axis=0)]
    all_gather x1, blocking collectives: 36.8 us -> 21 us  [local(): lax.all_gather(reduced.astype(jnp.bfloat16), 'dom', axis=0, tiled=True)]
    unnamed x3 -> x4, waiting for transfers between devices: 105 us -> 105 us
  transfers between devices with their start and end apart: 2 -> 3, of which waited for: 2 -> 3; matrix products, arithmetic and copies ran while one was open for 0% -> 0% of each run, Pallas kernels for 0% -> 0%
where the time goes in v2:
time: 505 us; the launch traced here: 504 us
  waiting for transfers between devices  410 us (81%)
  matrix products  24 us (5%)
  blocking collectives  21 us (4%)
  between operations  14.6 us (3%)
  local copies, waits for them, and re-layouts  13.8 us (3%)
  other arithmetic  11.6 us (2%)
  loops' own time  8.98 us (2%)
    psum x1, waiting for transfers between devices, local(): totals = lax.psum(totals, ('gz', 'dom'))  254 us
    unnamed x4, waiting for transfers between devices  105 us
    all_gather x1, waiting for transfers between devices, local(): reduced = jnp.sum(lax.all_gather(partial_slices, 'gz'), axis=0)  51.7 us
    all_gather x1, blocking collectives, local(): lax.all_gather(reduced.astype(jnp.bfloat16), 'dom', axis=0, tiled=True)  21 us
    dot_general x8, matrix products, extract(): jnp.dot(flat_volume, x_weights.T, precision=lax.Precision.HIGHEST, prefer...  11.5 us
  transfers between devices with their start and end apart: 3, of which 3 were waited for; matrix products, arithmetic and copies ran while one was open for 0% of the time, Pallas kernels for 0%

profile of v2, /device:TPU:1, one launch (start us, length us, event | category | flops | bytes accessed | tf_op | source)
XLA Modules:
  0.0 504.4 jit_solution(17906692954603817963)
XLA Ops:
  7.2 1.1 reshape.295
  8.3 29.3 %while.29 = (s32[]{:T(128)}, f32[8,8,384]{2,1,0:T(8,128)S(1)}, s32[8]{0:T(128)S(1)}, s32[]{:T(128)}, f32[192,384]{1,0:T(8,128)S(1)}, /*index=5*/s32[]{:T(128)}, s32[]{:T(128)}, f32[]{:T(128)}, f32[]{:T(128)}, f32[]{:T(128)}) while((s32[]{:T(128)}, f32[8,8,384]{2,1,0:T(8,128)S(1)}, s32[8]{0:T(128)S(1)}, s32[]{:T(128)}, ...), condition=%wide.region_3.4_spmd.clone, body=%wide.region_0.3_spmd.clone.sunk | while | flops 682043264 | bytes 5361225 | solution.py:82
  8.3 0.6 dynamic_slice.26
  9.8 0.3 fusion.88
  10.1 1.4 convolution_bitcast_fusion.2
  12.0 0.6 dynamic_slice.26
  13.4 0.3 fusion.88
  13.7 1.5 convolution_bitcast_fusion.2
  15.7 0.6 dynamic_slice.26
  17.1 0.3 fusion.88
  17.4 1.4 convolution_bitcast_fusion.2
  19.4 0.6 dynamic_slice.26
  21.1 1.4 convolution_bitcast_fusion.2
  23.0 0.6 dynamic_slice.26
  24.7 1.4 convolution_bitcast_fusion.2
  26.7 0.6 dynamic_slice.26
  28.4 1.4 convolution_bitcast_fusion.2
  30.3 0.6 dynamic_slice.26
  32.0 1.4 convolution_bitcast_fusion.2
  34.0 0.6 dynamic_slice.26
  35.4 0.3 fusion.88
  35.7 1.4 convolution_bitcast_fusion.2
  37.6 0.6 copy-done.2
  38.5 51.7 %all-gather.3.cloned.1.call-done = f32[128,8,384]{2,1,0:T(8,128)} async-done(((f32[8,8,384]{2,1,0:T(8,128)}), f32[128,8,384]{2,1,0:T(8,128)}) %all-gather.3.cloned.1.call-update) | async-done | bytes 1572880 | tf_op jit(solution)/shard_map/all_gather | solution.py:83
  90.2 1.5 reduce_sum.69
  91.7 21.0 %all_gather.11 = bf16[128,8,384]{2,1,0:T(8,128)(2,1)S(1)} all-gather(bf16[8,8,384]{2,1,0:T(8,128)(2,1)S(1)} %reduce_sum.69), channel_id=1, replica_groups=mesh['gz'=16,'dom'=16] {'dom'}, dimensions={0}, use_global_device_ids=true | all-gather | bytes 835584 | tf_op jit(solution)/shard_map/all_gather | solution.py:84
  112.8 0.6 copy.15
  113.4 0.3 fusion.58
  114.3 0.5 sqrt_multiply_fusion
  115.0 2.0 fusion.63
  117.1 254.0 %all-reduce.4.cloned.1.call-done = f32[128,3072]{1,0:T(8,128)} async-done(((f32[128,3072]{1,0:T(8,128)}), f32[128,3072]{1,0:T(8,128)}) %all-reduce.4.cloned.1.call-update) | async-done | bytes 1572880 | tf_op jit(solution)/shard_map/psum | solution.py:113
  371.1 0.9 constant_dynamic-slice_fusion.1
  372.0 17.9 %while.30 = (s32[]{:T(128)}, f32[192,384]{1,0:T(8,128)S(1)}, s32[]{:T(128)}, f32[8,8,384]{2,1,0:T(8,128)S(1)}, s32[]{:T(128)}, /*index=5*/s32[]{:T(128)}, f32[]{...) while((s32[]{:T(128)}, f32[192,384]{1,0:T(8,128)S(1)}, s32[]{:T(128)}, ...), condition=%wide.region_11.12_spmd.clone, body=%wide.region_10.11_spmd.clone.sunk | while | flops 682190720 | bytes 5656159 | solution.py:135
  372.7 0.3 fusion.94
  373.0 1.2 fusion.96
  375.3 1.2 fusion.96
  377.5 1.2 fusion.96
  379.7 1.2 fusion.96
  382.0 1.2 fusion.96
  383.9 0.3 fusion.94
  384.2 1.2 fusion.96
  386.2 0.3 fusion.94
  386.5 1.2 fusion.96
  388.7 1.2 fusion.96
  390.0 0.8 reshape.299
  390.8 0.6 dynamic-slice
  392.0 104.5 %all-reduce.6.cloned.1.call-done = f32[48,4,384]{2,1,0:T(4,128)} async-done(((f32[48,4,384]{2,1,0:T(4,128)}), f32[48,4,384]{2,1,0:T(4,128)}) %all-reduce.6.cloned.1.call-update) | async-done | bytes 294928
  496.6 1.3 constant_dynamic-slice_fusion
  (175 shorter events, 11.1 us)
Async XLA Ops:
  7.2 83.1 %all-gather.3.cloned.1.call-start = ((), (), s32[]{:S(2)}) async-start(), calls=%async_computation.1 | async-start | bytes 1671168 | tf_op jit(solution)/shard_map/all_gather | solution.py:83
  8.3 30.0 %copy-start.1 = (f32[32,2,384]{2,1,0:T(2,128)S(1)}, f32[32,2,384]{2,1,0:T(2,128)}, u32[]{:S(2)}) copy-start(f32[32,2,384]{2,1,0:T(2,128)} %param.11) | copy-start | bytes 294916
  8.3 30.0 %copy-start.4 = (s32[16]{0:T(128)S(1)}, s32[16]{0:T(128)}, u32[]{:S(2)}) copy-start(s32[16]{0:T(128)} %param.12) | copy-start | bytes 196
  37.6 0.6 copy-start.2
  38.3 332.9 %all-reduce.4.cloned.1.call-start = ((), (), s32[]{:S(2)}) async-start(), calls=%async_computation | async-start | bytes 3145728 | tf_op jit(solution)/shard_map/psum | solution.py:113
  91.7 21.6 %copy-start.3 = (s32[16]{0:T(128)S(1)}, s32[16]{0:T(128)}, u32[]{:S(2)}) copy-start(s32[16]{0:T(128)} %param.13) | copy-start | bytes 196
  112.8 0.9 copy-start
  117.0 379.5 %all-reduce.6.cloned.1.call-start = ((), (), s32[]{:S(2)}) async-start(), calls=%async_computation.2 | async-start | bytes 589824
  372.0 18.8 %copy-start.5 = (u32[256]{0:T(256)S(1)}, u32[256]{0:T(256)}, u32[]{:S(2)}) copy-start(u32[256]{0:T(256)} %constant.211) | copy-start | bytes 3076
Sparse Core Ops, SparseCore 0:
  38.4 51.8 all-gather.2
  117.2 253.9 all-reduce.3
  390.9 105.6 all-reduce.5
